TPU v7x, 128 devices: a whole 4x4x4 slice. The times are simulated.
128 devices in a mesh: chan: 8 (over x, z_hi), row: 4 (over y), col: 4 (over z_lo, core).
Axes of the slice: x: 4, y: 4, z: 4 (z_hi: 2, z_lo: 2; z = z_hi * 2 + z_lo), core: 2. Of those that a mesh axis runs over, the one named last changes fastest.
Arguments:
- voltages: bfloat16 [2, 4, 512, 64, 1031], P(None, None, ('chan', 'row', 'col')), may hold values from -6 to 6
- window: float32 [8, 64], replicated, may hold values from 0.1 to 0.6
- kept_channels: int32 [48], replicated, may hold values from 0 to 63, as said below
Outputs:
- covariance: float32 [48, 2, 2048, 2048], P('chan', None, 'row', 'col')
Inputs may be any that keep to these rules, and one draw needn't show every extreme that they name: `kept_channels`: 48 distinct channel numbers of the 64-point transform, in any order.
All inputs are finite; a program needn't handle non-finite values.
Results may differ from a plain program's by a relative error of at most 0.0019.
Values may be sent and summed in bfloat16 or wider, within the bound.
No kernel may reach another device: no remote copies, remote signals or barrier semaphores. Data moves between devices by JAX's collectives and lax.ppermute only.
A program may use at most 128 MiB of HBM per device.

v0:
```python
import math
import jax
import jax.numpy as jnp
from jax import lax
from jax.sharding import Mesh
from jax.sharding import PartitionSpec as P

COL = ("col_0", "col_1")
CHAN_ROW_COL = ("chan", "row", "col_0", "col_1")
ROW_COL = ("row", "col_0", "col_1")


def in_order(tiles, dim):
    shape = list(tiles.shape[1:])
    shape[dim] *= tiles.shape[0]
    return jnp.moveaxis(tiles, 0, dim).reshape(shape)


def gather_in_order(shard, axes, turns):
    tiles = shard[None]
    for k in turns:
        tiles = lax.all_gather(tiles, axes[k], axis=0, tiled=True)
    current = [lax.axis_size(axes[k]) for k in reversed(turns)]
    tiles = tiles.reshape(*current, *shard.shape)
    turned = sorted(range(len(turns)), key=lambda place: turns[len(turns) - 1 - place])
    return tiles.transpose(*turned, *range(len(turns), tiles.ndim)).reshape(-1, *shard.shape)


def whole_of(shard, axes, turns, dim):
    return in_order(gather_in_order(shard, axes, turns), dim)


def cut_along(shard, dim, peers):
    shape = shard.shape
    tiles = shard.reshape(*shape[:dim], peers, shape[dim] // peers, *shape[dim + 1 :])
    return jnp.moveaxis(tiles, dim, 0)


def exchange_both(shard, axis, axes, splits, concats):
    sizes = [lax.axis_size(a) for a in axes]
    tiles = cut_along(shard, splits[0], sizes[0])
    tiles = jnp.moveaxis(cut_along(tiles, splits[1] + 1, sizes[1]), 0, 1)
    inside = tiles.shape[2:]
    tiles = tiles.reshape(-1, *inside)
    tiles = lax.all_to_all(tiles, axis, split_axis=0, concat_axis=0, tiled=True)
    tiles = in_order(tiles.reshape(*sizes, *inside), concats[0] + 1)
    return in_order(tiles, concats[1])


def phase_table(kept_channels, points):
    positions = jnp.arange(points, dtype=jnp.int32)
    phases = kept_channels[:, None] * positions[None, :] % points
    angles = phases.astype(jnp.float32) * (2.0 * math.pi / points)
    factor = 1.0 / math.sqrt(points)
    cosines = jnp.cos(angles) * factor
    sines = jnp.sin(angles) * factor
    return jnp.stack([jnp.stack([cosines, -sines]), jnp.stack([sines, cosines])])


def filter_bank(samples, window, frames):
    filtered = window[0][:, None] * samples[..., 0:frames]
    for tap_index in range(1, window.shape[0]):
        filtered = (
            filtered + window[tap_index][:, None] * samples[..., tap_index : tap_index + frames]
        )
    return filtered


def products(row_full, col_full):
    real_part = jnp.einsum(
        "bpmif,bpmjf->mij", row_full, col_full, preferred_element_type=jnp.float32
    )
    imag_part = jnp.einsum(
        "bmif,bmjf->mij", row_full[:, 1], col_full[:, 0], preferred_element_type=jnp.float32
    )
    imag_part = imag_part - jnp.einsum(
        "bmif,bmjf->mij", row_full[:, 0], col_full[:, 1], preferred_element_type=jnp.float32
    )
    inverse = 1.0 / (row_full.shape[0] * row_full.shape[4])
    return jnp.stack([real_part, imag_part], axis=1) * inverse


def correlate(pieces):
    row_part, col_part = pieces
    row_full = whole_of(row_part, COL, (0, 1), 0)
    col_full = lax.all_gather(col_part, "row", axis=0, tiled=True)
    return products(row_full, col_full)


def arrange(spectra, shape):
    return (spectra.reshape(shape), jnp.swapaxes(spectra, 1, 2).reshape(shape))


def shards(voltages, window, kept_channels):
    chan_count = lax.axis_size("chan")
    row_count = lax.axis_size("row")
    col_count = lax.axis_size(COL)
    points = window.shape[1]
    frames = voltages.shape[4] - window.shape[0] + 1
    slot_inputs = voltages.shape[2]
    per_chan = kept_channels.shape[0] // chan_count
    block_frames = frames // col_count
    samples = voltages.astype(jnp.float32)
    filtered = filter_bank(samples, window, frames)
    filtered = filtered.reshape(2, row_count, slot_inputs, points, col_count, block_frames)
    table = phase_table(kept_channels, points).reshape(2, 2, chan_count, per_chan, points)
    spectra = jnp.einsum(
        "qrsnbf,qpckn->crbpksf", filtered, table, precision=lax.Precision.HIGHEST
    ).astype(jnp.bfloat16)
    sectioned_shape = (
        chan_count,
        row_count * col_count,
        2,
        per_chan,
        1,
        1,
        slot_inputs,
        block_frames,
    )
    outgoing = arrange(spectra, sectioned_shape)
    arrived = (
        exchange_both(outgoing[0], CHAN_ROW_COL, ("chan", ROW_COL), (0, 1), (4, 5)),
        exchange_both(outgoing[1], CHAN_ROW_COL, ("chan", ROW_COL), (0, 1), (4, 5)),
    )
    arrived = jax.tree.map(lambda piece: piece.reshape(1, 2, per_chan, -1, block_frames), arrived)
    return correlate(arrived)


def solution(mesh):
    finer = Mesh(
        mesh.devices.reshape(mesh.shape["chan"], mesh.shape["row"], 2, 2),
        ("chan", "row", "col_0", "col_1"),
    )
    placed = (P(None, None, CHAN_ROW_COL, None, None), P(), P())
    return jax.shard_map(
        shards, mesh=finer, in_specs=placed, out_specs=P("chan", None, "row", COL), check_vma=False
    )
```

profile of v0, /device:TPU:1, one launch (start us, length us, event | category | flops | bytes accessed | tf_op | source)
XLA Modules:
  0.0 426.3 jit_solution(12734910430916442310)
XLA Ops:
  6.5 0.0 all-gather.4.cloned.1.call-start
  6.5 0.7 mul.173
  7.3 0.1 copy.31
  7.4 1.0 slice_bitcast_fusion.19
  8.3 0.2 fusion.31
  8.5 3.5 convert_element_type.36
  12.0 16.8 %fusion.2 = f32[2,4,4,64,1024]{4,3,2,1,0:T(8,128)} fusion(f32[2,4,4,64,1031]{4,3,2,1,0:T(8,128)S(1)} %convert_element_type.36, f32[64]{0:T(128)S(1)} %get-tuple-element.14, f32[64]{0:T(128)S(1)} %get-tuple-element.15, f32[64]{0:T(128)S(1)} %get-tuple-element.9, f32[64]{0:T(128)S(1)} %get-tuple-element.10, f32[64]{0:T(128)S(1)} %get-tuple-element.11, ...), kind=kLoop, calls=%fused_computation.4 | loop fusion | flops 31457280 | bytes 75499520 | tf_op jit(solution)/shard_map/add | solution.py:64
  28.8 10.6 %reshape.151 = f32[2,4,4,64,4,256]{5,4,3,2,1,0:T(4,128)} reshape(f32[2,4,4,64,1024]{4,3,2,1,0:T(8,128)} %fusion.2) | data formatting | bytes 16777216 | tf_op jit(solution)/shard_map/reshape | solution.py:105
  39.4 9.3 %bitcast_convert_fusion = bf16[2,8,6,4,4,4,256]{6,1,5,4,3,2,0:T(8,128)(2,1)S(1)} fusion(f32[2,4,4,64,4,256,1,1]{5,4,3,2,1,0,7,6:T(4,128)} %bitcast.102, f32[1,1,8,6,64]{4,2,0,3,1:T(8,128)S(1)} %get-tuple-element.7, f32[1,1,8,6,64]{4,2,0,3,1:T(8,128)S(1)} %get-tuple-element.6, f32[1,1,8,6,64]{4,2,0,3,1:T(8,128)S(1)} %get-tuple-element.5), kind=kOutput, calls=%fused_computation.28 | convolution fusion | flops 2417528832 | bytes 11571200 | tf_op jit(solution)/shard_map/qrsnbf,qpckn->crbpksf/dot_general | solution.py:107
  48.7 2.4 copy.33
  51.1 52.5 %all_to_all.10 = bf16[128,1,1,2,6,1,1,4,256]{8,7,4,3,6,5,2,1,0:T(4,128)(2,1)S(1)} all-to-all(bf16[128,1,1,2,6,1,1,4,256]{8,7,4,3,6,5,2,1,0:T(4,128)(2,1)S(1)} %bitcast.101), channel_id=1, replica_groups=mesh['chan'=8,'row'=4,'col_0'=2,'col_1'=2] {'chan','row','col_0','col_1'}, dimensions={0} | all-to-all | bytes 6291456 | tf_op jit(solution)/shard_map/all_to_all | solution.py:45
  103.7 3.3 copy.35
  106.9 2.2 copy.36
  109.1 0.0 all-gather.4.cloned.1.call-update
  109.1 0.0 all-gather.6.cloned.1.call-start
  109.2 79.7 %all-gather.4.cloned.1.call-done = bf16[2,1,2,6,512,256]{5,4,3,2,1,0:T(8,128)(2,1)} async-done(((bf16[1,1,2,6,512,256]{5,4,3,2,1,0:T(8,128)(2,1)}), bf16[2,1,2,6,512,256]{5,4,3,2,1,0:T(8,128)(2,1)}) %all-gather.4.cloned.1.call-update) | async-done | bytes 6291472 | tf_op jit(solution)/shard_map/all_gather | solution.py:22
  188.9 0.0 all-gather.6.cloned.1.call-update
  188.9 0.0 all-gather.8.cloned.1.call-start
  188.9 2.4 copy.38
  191.4 50.3 %all_to_all.11 = bf16[128,1,1,2,6,1,1,4,256]{8,7,4,3,6,5,2,1,0:T(4,128)(2,1)S(1)} all-to-all(bf16[128,1,1,2,6,1,1,4,256]{8,7,4,3,6,5,2,1,0:T(4,128)(2,1)S(1)} %bitcast.99), channel_id=1, replica_groups=mesh['chan'=8,'row'=4,'col_0'=2,'col_1'=2] {'chan','row','col_0','col_1'}, dimensions={0} | all-to-all | bytes 6291456 | tf_op jit(solution)/shard_map/all_to_all | solution.py:45
  241.6 1.7 copy.40
  243.4 3.0 reshape_reshape.7
  246.4 0.0 all-gather.8.cloned.1.call-update
  246.4 0.0 all-gather.6.cloned.1.call-done
  246.5 10.8 %copy.37 = bf16[2,2,1,2,6,512,256]{6,5,3,4,1,0,2:T(8,128)(2,1)} copy(bf16[2,2,1,2,6,512,256]{6,5,4,3,0,1,2:T(8,128)(2,1)} %bitcast.91) | data formatting | bytes 25165824 | tf_op jit(solution)/shard_map/transpose | solution.py:26
  257.3 104.5 %all-gather.8.cloned.1.call-done = bf16[4,2,6,512,256]{4,3,2,1,0:T(8,128)(2,1)} async-done(((bf16[1,2,6,512,256]{4,3,2,1,0:T(8,128)(2,1)}), bf16[4,2,6,512,256]{4,3,2,1,0:T(8,128)(2,1)}) %all-gather.8.cloned.1.call-update) | async-done | bytes 12582928 | tf_op jit(solution)/shard_map/all_gather | solution.py:86
  361.8 10.6 %fusion.11 = f32[6,512,512,1]{2,1,0,3:T(8,128)} fusion(bf16[4,2,6,512,256]{4,3,2,1,0:T(8,128)(2,1)} %all-gather.8.cloned.1.call-done, bf16[4,2,6,512,256]{4,3,1,2,0:T(8,128)(2,1)} %bitcast.92), kind=kOutput, calls=%fused_computation.21 | convolution fusion | flops 3221225472 | bytes 18874368 | tf_op jit(solution)/shard_map/bmif,bmjf->mij/dot_general | solution.py:76
  372.4 15.0 %fusion.16 = f32[6,1,512,512]{3,2,0,1:T(8,128)} fusion(bf16[4,2,6,512,256]{4,3,1,2,0:T(8,128)(2,1)} %bitcast.93, bf16[4,2,6,512,256]{4,3,2,1,0:T(8,128)(2,1)} %all-gather.8.cloned.1.call-done), kind=kOutput, calls=%fused_computation.29 | convolution fusion | flops 6442450944 | bytes 31457280 | tf_op jit(solution)/shard_map/bpmif,bpmjf->mij/dot_general | solution.py:70
  387.4 0.0 copy-start
  387.4 12.6 %fusion.13 = f32[6,1,512,512]{3,2,0,1:T(8,128)} fusion(f32[6,512,512,1]{2,1,0,3:T(8,128)} %fusion.11, bf16[4,2,6,512,256]{4,3,2,1,0:T(8,128)(2,1)} %all-gather.8.cloned.1.call-done, bf16[4,2,6,512,256]{4,3,1,2,0:T(8,128)(2,1)} %bitcast.94), kind=kOutput, calls=%fused_computation.27 | convolution fusion | flops 3222798336 | bytes 25165824 | tf_op jit(solution)/shard_map/bmif,bmjf->mij/dot_general | solution.py:73
  400.0 0.0 copy-done
  400.0 8.9 %maximum_multiply_fusion = f32[6,2,512,512]{3,2,0,1:T(8,128)} fusion(f32[6,1,512,512]{3,2,0,1:T(8,128)} %fusion.13, f32[6,1,512,512]{3,2,0,1:T(8,128)S(1)} %copy-done), kind=kLoop, calls=%fused_computation | loop fusion | flops 6291456 | bytes 25165824 | tf_op jit(solution)/shard_map/mul | solution.py:80
  408.9 10.9 %copy.44 = f32[6,2,512,512]{3,2,1,0:T(8,128)} copy(f32[6,2,512,512]{3,2,0,1:T(8,128)} %maximum_multiply_fusion) | data formatting | bytes 25165824 | tf_op jit(solution)/shard_map/mul | solution.py:80
Async XLA Ops:
  6.5 182.3 %all-gather.4.cloned.1.call-start = ((), (), s32[]{:S(2)}) async-start(), calls=%async_computation.2 | async-start | bytes 9437184 | tf_op jit(solution)/shard_map/all_gather | solution.py:22
  109.1 137.3 %all-gather.6.cloned.1.call-start = ((), (), s32[]{:S(2)}) async-start(), calls=%async_computation.3 | async-start | bytes 18874368 | tf_op jit(solution)/shard_map/all_gather | solution.py:22
  188.9 172.9 %all-gather.8.cloned.1.call-start = ((), (), s32[]{:S(2)}) async-start(), calls=%async_computation.4 | async-start | bytes 15728640 | tf_op jit(solution)/shard_map/all_gather | solution.py:86
  387.4 12.6 %copy-start = (f32[6,1,512,512]{3,2,0,1:T(8,128)S(1)}, f32[6,1,512,512]{3,2,0,1:T(8,128)}, u32[]{:S(2)}) copy-start(f32[6,1,512,512]{3,2,0,1:T(8,128)} %fusion.16) | copy-start | bytes 18874372
Sparse Core Ops, SparseCore 0:
  109.2 79.5 all-gather.3
  190.5 28.9 all-gather.5
  246.6 115.1 all-gather.7
where the time goes:
time: 427 us; the launch traced here: 426 us
  waiting for transfers between devices  184 us (43%)
  blocking collectives  103 us (24%)
  local copies, waits for them, and re-layouts  49.1 us (11%)
  matrix products  47.5 us (11%)
  other arithmetic  29.4 us (7%)
  between operations  13.2 us (3%)
    all_gather x1, waiting for transfers between devices, correlate(): col_full = lax.all_gather(col_part, 'row', axis=0, tiled=True)  105 us
    all_to_all x2, blocking collectives, exchange_both(): tiles = lax.all_to_all(tiles, axis, split_axis=0, concat_axis=0, tiled=True)  103 us
    all_gather x2, waiting for transfers between devices, gather_in_order(): tiles = lax.all_gather(tiles, axes[k], axis=0, tiled=True)  79.7 us
    add x1, other arithmetic, filter_bank(): filtered + window[tap_index][:, None] * samples[..., tap_index:tap_index...  16.8 us
    dot_general x1, matrix products, products(): jnp.einsum('bpmif,bpmjf->mij', row_full, col_full, preferred_element_type...  15 us
    dot_general x1, matrix products, products(): jnp.einsum('bmif,bmjf->mij', row_full[:, 1], col_full[:, 0], preferred_el...  12.6 us
    mul x1, local copies, waits for them, and re-layouts, products(): return jnp.stack([real_part, imag_part], axis=1) * inverse  10.9 us
    transpose x1, local copies, waits for them, and re-layouts, gather_in_order(): tiles.transpose(*turned, *range(len(turns), tiles.ndim))  10.8 us
  transfers between devices with their start and end apart: 3, of which 2 were waited for; matrix products, arithmetic and copies ran while one was open for 4% of the time, Pallas kernels for 0%

commit v1 on v0

--- a/solution.py
+++ b/solution.py
@@ -83,7 +83,9 @@
 def correlate(pieces):
     row_part, col_part = pieces
     row_full = whole_of(row_part, COL, (0, 1), 0)
-    col_full = lax.all_gather(col_part, "row", axis=0, tiled=True)
+    col_full = jnp.concatenate(
+        lax.all_to_all(jnp.stack(lax.axis_size("row") * [col_part]), "row", 0, 0), 0
+    )
     return products(row_full, col_full)
 
 

time: 427 us -> 458 us (1.073)
  waiting for transfers between devices: 184 us -> 207 us
  starting transfers between devices: 0.08 us -> 6.56 us
  matrix products: 47.5 us -> 42.6 us
    all_to_all x0 -> x1, waiting for transfers between devices: none -> 127 us  [correlate(): lax.all_to_all(jnp.stack(lax.axis_size('row') * [col_part]), 'row', 0, 0)]
    all_gather x1 -> x0, waiting for transfers between devices: 105 us -> none  [correlate(): col_full = lax.all_gather(col_part, 'row', axis=0, tiled=True)]
    all_to_all x0 -> x1, starting transfers between devices: none -> 6.52 us  [correlate(): lax.all_to_all(jnp.stack(lax.axis_size('row') * [col_part]), 'row', 0, 0)]
  transfers between devices with their start and end apart: 3 -> 3, of which waited for: 2 -> 2; matrix products, arithmetic and copies ran while one was open for 4% -> 5% of each run, Pallas kernels for 0% -> 0%
where the time goes in v1:
time: 458 us; the launch traced here: 457 us
  waiting for transfers between devices  207 us (45%)
  blocking collectives  103 us (22%)
  local copies, waits for them, and re-layouts  53.4 us (12%)
  matrix products  42.6 us (9%)
  other arithmetic  31.3 us (7%)
  between operations  13.5 us (3%)
  starting transfers between devices  6.56 us (1%)
    all_to_all x1, waiting for transfers between devices, correlate(): lax.all_to_all(jnp.stack(lax.axis_size('row') * [col_part]), 'row', 0, 0)  127 us
    all_to_all x2, blocking collectives, exchange_both(): tiles = lax.all_to_all(tiles, axis, split_axis=0, concat_axis=0, tiled=True)  103 us
    all_gather x2, waiting for transfers between devices, gather_in_order(): tiles = lax.all_gather(tiles, axes[k], axis=0, tiled=True)  79.7 us
    add x1, other arithmetic, filter_bank(): filtered + window[tap_index][:, None] * samples[..., tap_index:tap_index...  16.8 us
    dot_general x1, matrix products, products(): jnp.einsum('bpmif,bpmjf->mij', row_full, col_full, preferred_element_type...  14.9 us
    dot_general x1, matrix products, products(): jnp.einsum('bmif,bmjf->mij', row_full[:, 1], col_full[:, 0], preferred_el...  10.9 us
    mul x1, local copies, waits for them, and re-layouts, products(): return jnp.stack([real_part, imag_part], axis=1) * inverse  10.9 us
    mul x1, other arithmetic, products(): return jnp.stack([real_part, imag_part], axis=1) * inverse  10.8 us
  transfers between devices with their start and end apart: 3, of which 2 were waited for; matrix products, arithmetic and copies ran while one was open for 5% of the time, Pallas kernels for 0%

profile of v1, /device:TPU:1, one launch (start us, length us, event | category | flops | bytes accessed | tf_op | source)
XLA Modules:
  0.0 457.1 jit_solution(256704139636883759)
XLA Ops:
  6.5 0.0 all-gather.3.cloned.1.call-start
  6.5 1.0 slice_bitcast_fusion.19
  7.5 3.5 convert_element_type.36
  11.0 16.8 %fusion = f32[2,4,4,64,1024]{4,3,2,1,0:T(8,128)} fusion(f32[2,4,4,64,1031]{4,3,2,1,0:T(8,128)S(1)} %convert_element_type.36, f32[64]{0:T(128)S(1)} %get-tuple-element.14, f32[64]{0:T(128)S(1)} %get-tuple-element.15, f32[64]{0:T(128)S(1)} %get-tuple-element.9, f32[64]{0:T(128)S(1)} %get-tuple-element.10, f32[64]{0:T(128)S(1)} %get-tuple-element.11, ...), kind=kLoop, calls=%fused_computation.2 | loop fusion | flops 31457280 | bytes 75499520 | tf_op jit(solution)/shard_map/add | solution.py:64
  27.8 0.0 copy-start
  27.8 10.6 %reshape.158 = f32[2,4,4,64,4,256]{5,4,3,2,1,0:T(4,128)} reshape(f32[2,4,4,64,1024]{4,3,2,1,0:T(8,128)} %fusion) | data formatting | bytes 16777216 | tf_op jit(solution)/shard_map/reshape | solution.py:107
  38.4 0.0 copy-done
  38.4 0.1 mul.173
  38.5 0.1 copy.30
  38.6 0.2 fusion.26
  38.8 9.3 %bitcast_convert_fusion = bf16[2,8,6,4,4,4,256]{6,1,5,4,3,2,0:T(8,128)(2,1)S(1)} fusion(f32[2,4,4,64,4,256,1,1]{5,4,3,2,1,0,7,6:T(4,128)} %bitcast.101, f32[1,1,8,6,64]{4,2,0,3,1:T(8,128)S(1)} %get-tuple-element.7, f32[1,1,8,6,64]{4,2,0,3,1:T(8,128)S(1)} %get-tuple-element.6, f32[1,1,8,6,64]{4,2,0,3,1:T(8,128)S(1)} %get-tuple-element.5), kind=kOutput, calls=%fused_computation.26 | convolution fusion | flops 2417528832 | bytes 11571200 | tf_op jit(solution)/shard_map/qrsnbf,qpckn->crbpksf/dot_general | solution.py:109
  48.1 2.4 copy.32
  50.5 52.5 %all_to_all.15 = bf16[128,1,1,2,6,1,1,4,256]{8,7,4,3,6,5,2,1,0:T(4,128)(2,1)S(1)} all-to-all(bf16[128,1,1,2,6,1,1,4,256]{8,7,4,3,6,5,2,1,0:T(4,128)(2,1)S(1)} %bitcast.100), channel_id=1, replica_groups=mesh['chan'=8,'row'=4,'col_0'=2,'col_1'=2] {'chan','row','col_0','col_1'}, dimensions={0} | all-to-all | bytes 6291456 | tf_op jit(solution)/shard_map/all_to_all | solution.py:45
  103.0 3.3 copy.34
  106.3 2.2 copy.35
  108.5 0.0 all-gather.3.cloned.1.call-update
  108.5 0.0 all-gather.5.cloned.1.call-start
  108.5 79.7 %all-gather.3.cloned.1.call-done = bf16[2,1,2,6,512,256]{5,4,3,2,1,0:T(8,128)(2,1)} async-done(((bf16[1,1,2,6,512,256]{5,4,3,2,1,0:T(8,128)(2,1)}), bf16[2,1,2,6,512,256]{5,4,3,2,1,0:T(8,128)(2,1)}) %all-gather.3.cloned.1.call-update) | async-done | bytes 6291472 | tf_op jit(solution)/shard_map/all_gather | solution.py:22
  188.2 0.0 all-gather.5.cloned.1.call-update
  188.3 2.4 copy.37
  190.7 50.3 %all_to_all.16 = bf16[128,1,1,2,6,1,1,4,256]{8,7,4,3,6,5,2,1,0:T(4,128)(2,1)S(1)} all-to-all(bf16[128,1,1,2,6,1,1,4,256]{8,7,4,3,6,5,2,1,0:T(4,128)(2,1)S(1)} %bitcast.97), channel_id=1, replica_groups=mesh['chan'=8,'row'=4,'col_0'=2,'col_1'=2] {'chan','row','col_0','col_1'}, dimensions={0} | all-to-all | bytes 6291456 | tf_op jit(solution)/shard_map/all_to_all | solution.py:45
  241.0 3.3 copy.39
  244.2 0.5 copy.40
  244.8 6.3 %stack.30 = bf16[4,1,2,6,512,256]{5,4,2,3,1,0:T(8,128)(2,1)} broadcast(bf16[2,6,512,256]{3,2,0,1:T(8,128)(2,1)S(1)} %copy.40), dimensions={2,3,4,5} | broadcast | bytes 15728640 | tf_op jit(solution)/shard_map/stack | solution.py:87
  251.0 6.5 %all-to-all-start.2 = ((bf16[4,1,2,6,512,256]{5,4,2,3,1,0:T(8,128)(2,1)}), bf16[4,1,2,6,512,256]{5,4,2,3,1,0:T(8,128)(2,1)}, u32[]{:S(2)}, u32[]{:S(2)}) async-start(bf16[4,1,2,6,512,256]{5,4,2,3,1,0:T(8,128)(2,1)} %stack.30), calls=%async_computation.2 | async-start | bytes 25165824 | tf_op jit(solution)/shard_map/all_to_all | solution.py:87
  257.6 0.0 all-gather.5.cloned.1.call-done
  257.6 10.5 %copy.36 = bf16[2,2,1,2,6,512,256]{6,5,3,4,1,0,2:T(8,128)(2,1)} copy(bf16[2,2,1,2,6,512,256]{6,5,4,3,0,1,2:T(8,128)(2,1)} %bitcast.89) | data formatting | bytes 25165824 | tf_op jit(solution)/shard_map/transpose | solution.py:26
  268.1 127.2 %all-to-all-done.2 = bf16[4,1,2,6,512,256]{5,4,2,3,1,0:T(8,128)(2,1)} async-done(((bf16[4,1,2,6,512,256]{5,4,2,3,1,0:T(8,128)(2,1)}), bf16[4,1,2,6,512,256]{5,4,2,3,1,0:T(8,128)(2,1)}, u32[]{:S(2)}, u32[]{:S(2)}) %all-to-all-start.2) | async-done | bytes 12582944 | tf_op jit(solution)/shard_map/all_to_all | solution.py:87
  395.2 7.5 %fusion.9 = f32[6,512,512,1]{2,1,0,3:T(8,128)S(1)} fusion(bf16[4,2,6,512,256]{4,3,1,2,0:T(8,128)(2,1)} %bitcast.32, bf16[4,2,6,512,256]{4,3,1,2,0:T(8,128)(2,1)} %bitcast.90), kind=kOutput, calls=%fused_computation.19 | convolution fusion | flops 3221225472 | bytes 18874368 | tf_op jit(solution)/shard_map/bmif,bmjf->mij/dot_general | solution.py:76
  402.7 10.9 %fusion.11 = f32[6,1,512,512]{3,2,0,1:T(8,128)} fusion(f32[6,512,512,1]{2,1,0,3:T(8,128)S(1)} %fusion.9, bf16[4,2,6,512,256]{4,3,1,2,0:T(8,128)(2,1)} %bitcast.32, bf16[4,2,6,512,256]{4,3,1,2,0:T(8,128)(2,1)} %bitcast.91), kind=kOutput, calls=%fused_computation.25 | convolution fusion | flops 3222798336 | bytes 25165824 | tf_op jit(solution)/shard_map/bmif,bmjf->mij/dot_general | solution.py:73
  413.6 14.9 %convolution_bitcast_fusion = f32[6,1,512,512]{3,2,0,1:T(8,128)} fusion(bf16[4,2,6,512,256]{4,3,1,2,0:T(8,128)(2,1)} %bitcast.92, bf16[4,1,2,6,512,256]{5,4,2,3,1,0:T(8,128)(2,1)} %all-to-all-done.2), kind=kOutput, calls=%fused_computation.27 | convolution fusion | flops 6442450944 | bytes 31457280 | tf_op jit(solution)/shard_map/bpmif,bpmjf->mij/dot_general | solution.py:70
  428.5 10.8 %maximum_multiply_fusion = f32[6,2,512,512]{3,2,0,1:T(8,128)} fusion(f32[6,1,512,512]{3,2,0,1:T(8,128)} %fusion.11, f32[6,1,512,512]{3,2,0,1:T(8,128)} %convolution_bitcast_fusion), kind=kLoop, calls=%fused_computation | loop fusion | flops 6291456 | bytes 25165824 | tf_op jit(solution)/shard_map/mul | solution.py:80
  439.4 10.9 %copy.41 = f32[6,2,512,512]{3,2,1,0:T(8,128)} copy(f32[6,2,512,512]{3,2,0,1:T(8,128)} %maximum_multiply_fusion) | data formatting | bytes 25165824 | tf_op jit(solution)/shard_map/mul | solution.py:80
Async XLA Ops:
  6.5 181.7 %all-gather.3.cloned.1.call-start = ((), (), s32[]{:S(2)}) async-start(), calls=%async_computation.3 | async-start | bytes 9437184 | tf_op jit(solution)/shard_map/all_gather | solution.py:22
  27.8 10.6 %copy-start = (s32[48]{0:T(128)S(1)}, s32[48]{0:T(128)}, u32[]{:S(2)}) copy-start(s32[48]{0:T(128)} %param.5) | copy-start | bytes 580
  108.5 149.1 %all-gather.5.cloned.1.call-start = ((), (), s32[]{:S(2)}) async-start(), calls=%async_computation.4 | async-start | bytes 18874368 | tf_op jit(solution)/shard_map/all_gather | solution.py:22
  251.0 144.2 %all-to-all-start.2 = ((bf16[4,1,2,6,512,256]{5,4,2,3,1,0:T(8,128)(2,1)}), bf16[4,1,2,6,512,256]{5,4,2,3,1,0:T(8,128)(2,1)}, u32[]{:S(2)}, u32[]{:S(2)}) async-start(bf16[4,1,2,6,512,256]{5,4,2,3,1,0:T(8,128)(2,1)} %stack.30), calls=%async_computation.2 | async-start | bytes 25165824 | tf_op jit(solution)/shard_map/all_to_all | solution.py:87
Sparse Core Ops, SparseCore 0:
  108.6 79.5 all-gather.2
  189.9 28.9 all-gather.4
